TPU v7x, 256 devices: a whole 4x4x8 slice. The times are simulated.
256 devices in a mesh: gx: 4 (over z_lo, core), gy: 4 (over z_hi), gz: 16 (over y, x).
Axes of the slice: x: 4, y: 4, z: 8 (z_hi: 4, z_lo: 2; z = z_hi * 2 + z_lo), core: 2. Of those that a mesh axis runs over, the one named last changes fastest.
Arguments:
- parts: float32 [52, 52, 112, 128], P('gx', 'gy', 'gz'), may hold values from -6 to 6
- cell_matrix: bfloat16 [343, 343], replicated, may hold values from -0.2 to 2
- cell_potential: float32 [343, 8, 8, 16], P(None, 'gx', 'gy', 'gz'), may hold values from 0 to 1
- projectors: bfloat16 [4, 4, 16, 343, 1536], P('gx', 'gy', 'gz'), may hold values from -0.15625 to 0.15625
- slot_atom: int32 [4, 4, 16, 32], P('gx', 'gy'), may hold values from -1 to 63, as said below
- slot_cells: int32 [4, 4, 16, 32, 4], P('gx', 'gy', 'gz'), may hold values from 0 to 3
- coupling: float32 [1024, 12, 12], P(('gx', 'gy')), may hold values from -1.75 to 1.75
Outputs:
- filtered: float32 [52, 52, 112, 128], P('gx', 'gy', 'gz')
Inputs may be any that keep to these rules, and one draw needn't show every extreme that they name: `slot_atom`: entry s of partition (i, j, k) is -1 (an empty slot) or the number, within the column (i, j), of an atom whose projectors reach into that partition. Slots c * 2 to c * 2 + 1 of every partition hold only atoms numbered c * 4 to c * 4 + 3, which are owned by partition c of the column along gz. An atom stands at most once in one partition's list.
All inputs are finite; a program needn't handle non-finite values.
Results may differ from a plain program's by a relative error of at most 0.0058.
Values may be sent and summed in bfloat16 or wider, within the bound.
A program may use at most 64 MiB of HBM per device.

v0:
```python
import jax
import jax.numpy as jnp
from jax import lax
from jax.experimental import pallas as pl
from jax.experimental.pallas import tpu as pltpu
from jax.sharding import PartitionSpec as P

ORDER = 6
STEPS = 3
PA = 12
POS = 32
BLK = 4
CELLS = 4

EDGE = ORDER + 1
NODES = EDGE**3
WIDE = 2 * ORDER + 1
SUB = 8
LANES = 128
ROW = WIDE * SUB
FIELD = WIDE * ROW
TALL = 1408
CROWS = 400
KPAD = 512
SLOT = 16
COLS = POS * SLOT
GROUP = 8 * SLOT
PGROUP = 8 * BLK * PA

center_value = 2.0
half_width = 3.0

MESH = pl.DeviceIdType.MESH
BF = jnp.bfloat16
F32 = jnp.float32

FACES = [(1, 0, 0), (-1, 0, 0), (0, 1, 0), (0, -1, 0), (0, 0, 1), (0, 0, -1)]
XY = [(a, b, 0) for a in (-1, 1) for b in (-1, 1)]
XZ = [(a, 0, b) for a in (-1, 1) for b in (-1, 1)]
YZ = [(0, a, b) for a in (-1, 1) for b in (-1, 1)]
CORNERS = [(a, b, c) for a in (-1, 1) for b in (-1, 1) for c in (-1, 1)]
DIRS = CORNERS + XY + YZ + FACES + XZ


def region_rows(d):
    if d[2] != 0 and d[0] == 0 and d[1] == 0:
        return 176
    if sum(1 for x in d if x != 0) == 1:
        return 112
    return 16


OFFSET = {}
_total = 0
for _d in DIRS:
    OFFSET[_d] = _total
    _total += region_rows(_d)
HALO_ROWS = _total


def side(step, last):
    return last if step > 0 else 0


def iota(shape, axis):
    return lax.broadcasted_iota(jnp.int32, shape, axis)


def dot(a, b):
    return jnp.dot(a, b, preferred_element_type=F32)


def dot_nt(a, b):
    return lax.dot_general(a, b, (((1,), (1,)), ((), ())), preferred_element_type=F32)


def onehot(mask):
    return jnp.where(mask, 1.0, 0.0).astype(BF)


def body(sizes, parts, amat, pot, proj, atoms, cells, coup, out,
         zbuf, field, ybuf, xcat, qt, q, a2, vloc, gmat, csc,
         part_send, part_recv, coef_send, coef_recv, halo_send, halo_recv,
         hsend_sem, hrecv_sem, psend_sem, precv_sem, csend_sem, crecv_sem):
    ngx, ngy, ngz = sizes
    ix, iy, iz = lax.axis_index("gx"), lax.axis_index("gy"), lax.axis_index("gz")
    cap = POS // ngz
    own = coup.shape[0] // ngz
    chunk = cap * SLOT

    def exists(d, sign):
        ok = None
        for pos, size, step in ((ix, ngx, d[0]), (iy, ngy, d[1]), (iz, ngz, d[2])):
            if step == 0:
                continue
            c = (pos + 1 < size) if step * sign > 0 else (pos > 0)
            ok = c if ok is None else jnp.logical_and(ok, c)
        return ok

    def target(d):
        return (ix + d[0], iy + d[1], iz + d[2])

    def peer(k):
        return lax.rem(iz + k, ngz)

    halo_recv[...] = jnp.zeros(halo_recv.shape, BF)
    barrier = pltpu.get_barrier_semaphore()
    for d in DIRS:
        @pl.when(exists(d, 1))
        def _(d=d):
            pl.semaphore_signal(barrier, inc=1, device_id=target(d), device_id_type=MESH)

    def greet(k, carry):
        pl.semaphore_signal(barrier, inc=1, device_id=(ix, iy, peer(k)), device_id_type=MESH)
        return carry

    lax.fori_loop(1, ngz, greet, 0)

    def span(pos, size):
        return 1 + (pos > 0).astype(jnp.int32) + (pos + 1 < size).astype(jnp.int32)

    n_greet = span(ix, ngx) * span(iy, ngy) * span(iz, ngz) - 1 + ngz - 1

    zero8 = jnp.zeros((SUB, LANES), F32)
    field[FIELD:, :] = jnp.zeros((TALL - FIELD, LANES), F32)
    ybuf[...] = jnp.zeros(ybuf.shape, F32)

    def take(u, carry):
        for v in range(WIDE):
            at = pl.multiple_of(u * ROW, SUB) + v * SUB
            tile = jnp.concatenate([parts[u, v], jnp.zeros((1, LANES), F32)], axis=0)
            field[pl.ds(at, SUB), :] = tile
        return carry

    lax.fori_loop(0, WIDE, take, 0)

    def halo_copy(d, slot):
        source = (d[0], d[1], 0) if d in CORNERS else d
        n = region_rows(d)
        k = DIRS.index(d)
        return pltpu.make_async_remote_copy(
            src_ref=halo_send.at[pl.ds(OFFSET[source], n)],
            dst_ref=halo_recv.at[slot, pl.ds(OFFSET[d], n)],
            send_sem=hsend_sem.at[k],
            recv_sem=hrecv_sem.at[slot, k],
            device_id=target(d),
            device_id_type=MESH,
        )

    def pack():
        def put(d, value):
            halo_send[pl.ds(OFFSET[d], region_rows(d)), :] = value.astype(BF)

        for d in XY:
            at = side(d[0], WIDE - 1) * ROW + side(d[1], WIDE - 1) * SUB
            put(d, jnp.concatenate([field[pl.ds(at, SUB), :], zero8], axis=0))
        for d in FACES:
            if d[0] != 0:
                at = side(d[0], WIDE - 1) * ROW
                put(d, jnp.concatenate([field[pl.ds(at, ROW), :], zero8], axis=0))
            elif d[1] != 0:
                v = side(d[1], WIDE - 1)
                value = jnp.concatenate(
                    [field[pl.ds(u * ROW + v * SUB, SUB), :] for u in range(WIDE)], axis=0)
                ybuf[pl.ds(side(d[1], 1) * LANES, ROW), :] = value
                put(d, jnp.concatenate([value, zero8], axis=0))
            else:
                put(d, field[pl.ds(side(d[2], ORDER), 176, stride=SUB), :])
        for d in YZ:
            put(d, ybuf[pl.ds(side(d[1], 1) * LANES + side(d[2], ORDER), 16, stride=SUB), :])
        for d in XZ:
            at = side(d[0], WIDE - 1) * ROW + side(d[2], ORDER)
            put(d, field[pl.ds(at, 16, stride=SUB), :])

    def halo_start(slot):
        for d in DIRS:
            @pl.when(exists(d, 1))
            def _(d=d):
                halo_copy(d, slot).start()

    def halo_wait(slot):
        for d in DIRS:
            @pl.when(exists(d, -1))
            def _(d=d):
                halo_copy(d, slot).wait_recv()
        for d in DIRS:
            @pl.when(exists(d, 1))
            def _(d=d):
                halo_copy(d, slot).wait_send()

    def unpack(slot):
        def got(d):
            return halo_recv[slot, pl.ds(OFFSET[d], region_rows(d)), :].astype(F32)

        def other(step, last):
            return 0 if step > 0 else last

        keep = iota((16, LANES), 0) < WIDE
        for d in FACES:
            if d[0] != 0:
                at = pl.ds(other(d[0], WIDE - 1) * ROW, ROW)
                field[at, :] = field[at, :] + got(d)[:ROW]
            elif d[1] != 0:
                v = other(d[1], WIDE - 1)
                ybuf[pl.ds(0, ROW), :] = got(d)[:ROW]
                for dz in (-1, 1):
                    rows = pl.ds(other(dz, ORDER), 16, stride=SUB)
                    ybuf[rows, :] = ybuf[rows, :] + got((0, d[1], dz))
                for u in range(WIDE):
                    at = pl.ds(u * ROW + v * SUB, SUB)
                    field[at, :] = field[at, :] + ybuf[pl.ds(u * SUB, SUB), :]
            else:
                rows = pl.ds(other(d[2], ORDER), 176, stride=SUB)
                field[rows, :] = field[rows, :] + got(d)
        for d in XZ:
            rows = pl.ds(other(d[0], WIDE - 1) * ROW + other(d[2], ORDER), 16, stride=SUB)
            field[rows, :] = field[rows, :] + jnp.where(keep, got(d), 0.0)
        for d in XY:
            base = other(d[0], WIDE - 1) * ROW + other(d[1], WIDE - 1) * SUB
            at = pl.ds(base, SUB)
            total = field[at, :] + got(d)[:SUB]
            field[at, :] = total
            first = got((d[0], d[1], 1))[ORDER:EDGE]
            last = got((d[0], d[1], -1))[:1]
            field[pl.ds(base, 1), :] = field[pl.ds(base, 1), :] + first
            field[pl.ds(base + ORDER, 1), :] = field[pl.ds(base + ORDER, 1), :] + last

    def split_cells(values):
        xs = []
        for p in range(2):
            for r in range(2):
                pieces = [
                    values[(ORDER * p + a) * ROW + ORDER * SUB * r:
                           (ORDER * p + a) * ROW + ORDER * SUB * r + EDGE * SUB]
                    for a in range(EDGE)]
                xs.append(jnp.concatenate(pieces + [zero8], axis=0))
        return xs

    def join_cells(blocks):
        rows = []
        for u in range(WIDE):
            halves = []
            for r in range(2):
                value = None
                for p in range(2):
                    a = u - ORDER * p
                    if 0 <= a <= ORDER:
                        piece = blocks[2 * p + r][a * EDGE * SUB:(a + 1) * EDGE * SUB]
                        value = piece if value is None else value + piece
                halves.append(value)
            left, right = halves
            cut = ORDER * SUB
            rows.append(jnp.concatenate(
                [left[:cut], left[cut:] + right[:SUB], right[SUB:]], axis=0))
        return rows

    pack()
    pl.semaphore_wait(barrier, n_greet)
    halo_start(0)

    r_i, n_i = iota((KPAD, NODES), 0), iota((KPAD, NODES), 1)
    expand = onehot(jnp.logical_and(
        jnp.logical_and(r_i < EDGE * EDGE * SUB, (r_i & 7) < EDGE),
        n_i == (r_i >> 3) * EDGE + (r_i & 7)))
    short = expand[:CROWS]
    a2[...] = dot_nt(dot(short, amat[...]).astype(BF), expand).astype(BF)

    wide_pot = jnp.concatenate(
        [jnp.broadcast_to(pot[:, g:g + 1], (NODES, LANES)) for g in range(CELLS)], axis=1)
    v_cells = jnp.dot(short.astype(F32), wide_pot, precision=lax.Precision.HIGHEST,
                      preferred_element_type=F32)
    for u, row in enumerate(join_cells(
            [v_cells[:, g * LANES:(g + 1) * LANES] for g in range(CELLS)])):
        vloc[pl.ds(u * ROW, ROW), :] = row

    width = POS * BLK * PA
    s_i, col = iota((POS, width), 0), iota((POS, width), 1)
    cell_f = cells[...].astype(F32)
    cell_col = jnp.zeros((1, width), F32)
    for b in range(BLK):
        start = s_i * (BLK * PA) + b * PA
        inside = jnp.logical_and(col >= start, col < start + PA)
        cell_col = cell_col + jnp.sum(
            jnp.where(inside, jnp.broadcast_to(cell_f[:, b:b + 1], (POS, width)), 0.0),
            axis=0, keepdims=True)
    in_slot = onehot(jnp.logical_and(col >= s_i * (BLK * PA), col < (s_i + 1) * (BLK * PA)))
    atom_bf = atoms[...].astype(F32).astype(BF)
    atom_all = dot(atom_bf, in_slot)
    atom_col = jnp.sum(jnp.where(iota((ngz, width), 0) == iz, atom_all, 0.0),
                       axis=0, keepdims=True)

    wide_proj = dot(expand, proj[...])
    rr, rc = iota((PGROUP, GROUP), 0), iota((PGROUP, GROUP), 1)
    tr, tc = iota((GROUP, PGROUP), 1), iota((GROUP, PGROUP), 0)

    def merge(row, column):
        base = (column >> 4) * (BLK * PA) + (column & 15)
        hit = row == base
        for b in range(1, BLK):
            hit = jnp.logical_or(hit, row == base + b * PA)
        return onehot(jnp.logical_and(hit, (column & 15) < PA))

    narrow, narrow_t = merge(rr, rc), merge(tr, tc)
    for g in range(CELLS):
        live = jnp.logical_and(cell_col == g, atom_col >= 0.0)
        masked = jnp.where(live, wide_proj, 0.0).astype(BF)
        for k in range(POS // 8):
            piece = masked[:, k * PGROUP:(k + 1) * PGROUP]
            q[pl.ds(g * CROWS, CROWS), pl.ds(k * GROUP, GROUP)] = dot(
                piece[:CROWS], narrow).astype(BF)
            qt[pl.ds(k * GROUP, GROUP), pl.ds(g * KPAD, KPAD)] = dot_nt(
                narrow_t, piece).astype(BF)

    at_s, at_c = iota((POS, COLS), 0), iota((POS, COLS), 1)
    j_c = lax.rem(at_c >> 4, cap)
    src = onehot(at_s == iz * cap + j_c)
    got_atoms = dot(atom_bf, src)
    k_r, k_c = iota((ngz, COLS), 0), iota((ngz, COLS), 1)
    here = jnp.logical_and(k_c >= k_r * chunk, k_c < (k_r + 1) * chunk)
    atom_row = jnp.sum(jnp.where(here, got_atoms, 0.0), axis=0, keepdims=True)
    m_r, m_c = iota((LANES, COLS), 0), iota((LANES, COLS), 1)
    same = jnp.logical_and((m_r & 15) == (m_c & 15), (m_r & 15) < PA)
    number = (m_r >> 4).astype(F32)
    base_atom = (iz * own).astype(F32)
    member = onehot(jnp.logical_and(
        same, jnp.broadcast_to(atom_row, (LANES, COLS)) - base_atom == number))
    member_t = dot_nt(onehot(iota((COLS, COLS), 0) == iota((COLS, COLS), 1)),
                      member).astype(BF)
    csc[...] = jnp.zeros(csc.shape, F32)
    for m in range(own):
        csc[pl.ds(m * SLOT, PA), pl.ds(0, PA)] = coup[iz * own + m]
    c_r, c_c = iota((LANES, LANES), 0), iota((LANES, LANES), 1)
    spread = onehot(jnp.logical_and(c_r == (c_c & 15), (c_c & 15) < PA))
    diagonal = (c_r >> 4) == (c_c >> 4)
    whole = csc[...]
    high = whole.astype(BF)
    low = (whole - high.astype(F32)).astype(BF)
    for h, piece in enumerate((high, low)):
        block = jnp.where(diagonal, dot(piece, spread), 0.0).astype(BF)
        gmat[h] = dot(dot(member_t, block).astype(BF), member).astype(BF)

    xcat[CROWS:, :] = jnp.zeros((KPAD - CROWS, CELLS * LANES), BF)
    zbuf[1] = jnp.zeros((FIELD, LANES), F32)

    halo_wait(0)
    unpack(0)
    zbuf[0] = field[pl.ds(0, FIELD), :]
    for g, value in enumerate(split_cells(field[pl.ds(0, FIELD), :])):
        xcat[pl.ds(0, CROWS), pl.ds(g * LANES, LANES)] = value.astype(BF)

    def exchange(src, dst, send_sem, recv_sem, k):
        to = peer(k)
        return pltpu.make_async_remote_copy(
            src_ref=src.at[pl.ds(pl.multiple_of(to * chunk, chunk), chunk)],
            dst_ref=dst.at[pl.ds(pl.multiple_of(iz * chunk, chunk), chunk)],
            send_sem=send_sem.at[k],
            recv_sem=recv_sem.at[k],
            device_id=(ix, iy, to),
            device_id_type=MESH,
        )

    def start_all(src, dst, send_sem, recv_sem):
        def go(k, carry):
            exchange(src, dst, send_sem, recv_sem, k).start()
            return carry

        lax.fori_loop(1, ngz, go, 0)
        mine = pl.ds(pl.multiple_of(iz * chunk, chunk), chunk)
        dst[mine, :] = src[mine, :]

    def wait_all(src, dst, send_sem, recv_sem):
        def go(k, carry):
            exchange(src, dst, send_sem, recv_sem, k).wait()
            return carry

        lax.fori_loop(1, ngz, go, 0)

    def step(t, carry):
        slot = lax.rem(t + 1, 2)
        now = lax.rem(t, 2)
        scale = jnp.where(t == 0, 1.0, 2.0) / half_width

        total = None
        for g in range(CELLS):
            term = dot(qt[:, g * KPAD:(g + 1) * KPAD], xcat[:, g * LANES:(g + 1) * LANES])
            total = term if total is None else total + term
        part_send[...] = total.astype(BF)
        start_all(part_send, part_recv, psend_sem, precv_sem)

        stiff = dot(a2[...], xcat[...])
        rows = join_cells([stiff[:, g * LANES:(g + 1) * LANES] for g in range(CELLS)])
        for u, row in enumerate(rows):
            at = pl.ds(u * ROW, ROW)
            field[at, :] = row + vloc[at, :] * zbuf[now, at, :]

        wait_all(part_send, part_recv, psend_sem, precv_sem)
        received = part_recv[...]
        coef_send[...] = (dot(gmat[0], received) + dot(gmat[1], received)).astype(BF)
        start_all(coef_send, coef_recv, csend_sem, crecv_sem)
        wait_all(coef_send, coef_recv, csend_sem, crecv_sem)

        coef = coef_recv[...]
        spread_cells = [dot(q[pl.ds(g * CROWS, CROWS), :], coef) for g in range(CELLS)]
        for u, row in enumerate(join_cells(spread_cells)):
            at = pl.ds(u * ROW, ROW)
            field[at, :] = field[at, :] + row

        pack()
        halo_start(slot)
        halo_wait(slot)
        unpack(slot)
        new = (field[pl.ds(0, FIELD), :] - center_value * zbuf[now]) * scale - zbuf[slot]
        zbuf[slot] = new
        for g, value in enumerate(split_cells(new)):
            xcat[pl.ds(0, CROWS), pl.ds(g * LANES, LANES)] = value.astype(BF)
        return carry

    lax.fori_loop(0, STEPS, step, 0)

    def give(u, carry):
        for v in range(WIDE):
            at = pl.multiple_of(u * ROW, SUB) + v * SUB
            out[u, v] = zbuf[STEPS % 2, pl.ds(at, SUB), :][:EDGE]
        return carry

    lax.fori_loop(0, WIDE, give, 0)


def local(sizes, parts, cell_matrix, cell_potential, projectors, slot_atom, slot_cells, coupling):
    ngz = sizes[2]

    def kernel(*refs):
        body(sizes, *refs)

    vm = pltpu.VMEM
    dma = pltpu.SemaphoreType.DMA
    n = len(DIRS)
    return pl.pallas_call(
        kernel,
        out_shape=jax.ShapeDtypeStruct(parts.shape, F32),
        in_specs=[pl.BlockSpec(memory_space=pltpu.VMEM)] * 7,
        out_specs=pl.BlockSpec(memory_space=pltpu.VMEM),
        scratch_shapes=[
            vm((2, FIELD, LANES), F32),
            vm((TALL, LANES), F32),
            vm((2 * LANES, LANES), F32),
            vm((KPAD, CELLS * LANES), BF),
            vm((COLS, CELLS * KPAD), BF),
            vm((CELLS * CROWS, COLS), BF),
            vm((CROWS, KPAD), BF),
            vm((FIELD, LANES), F32),
            vm((2, COLS, COLS), BF),
            vm((LANES, LANES), F32),
            vm((COLS, LANES), BF),
            vm((COLS, LANES), BF),
            vm((COLS, LANES), BF),
            vm((COLS, LANES), BF),
            vm((HALO_ROWS, LANES), BF),
            vm((2, HALO_ROWS, LANES), BF),
            dma((n,)),
            dma((2, n)),
            dma((ngz,)),
            dma((ngz,)),
            dma((ngz,)),
            dma((ngz,)),
        ],
        compiler_params=pltpu.CompilerParams(
            collective_id=0, has_side_effects=True, vmem_limit_bytes=56 * 1024 * 1024),
    )(
        parts,
        cell_matrix,
        cell_potential.reshape(NODES, CELLS),
        projectors.reshape(NODES, POS * BLK * PA),
        slot_atom.reshape(ngz, POS),
        slot_cells.reshape(POS, BLK),
        coupling,
    )


def solution(mesh):
    sizes = tuple(mesh.shape[a] for a in ("gx", "gy", "gz"))

    def run(*args):
        return local(sizes, *args)

    in_specs = (
        P("gx", "gy", "gz", None),
        P(),
        P(None, "gx", "gy", "gz"),
        P("gx", "gy", "gz", None, None),
        P("gx", "gy", None, None),
        P("gx", "gy", "gz", None, None),
        P(("gx", "gy"), None, None),
    )
    out_specs = P("gx", "gy", "gz", None)
    return jax.shard_map(run, mesh=mesh, in_specs=in_specs, out_specs=out_specs, check_vma=False)
```

profile of v0, /device:TPU:1, one launch (start us, length us, event | category | flops | bytes accessed | tf_op | source)
XLA Modules:
  0.0 82.9 jit_solution(13212650569298779618)
XLA Ops:
  0.0 0.7 reduce
  0.7 1.4 %copy.12.refs_5_ = s32[32,4]{1,0:T(8,128)} copy(s32[32,4]{0,1:T(4,128)} %bitcast.7) | data formatting | bytes 1024 | tf_op jit(solution)/shard_map/reshape | solution.py:475
  2.1 0.8 copy.11.refs_2_
  2.9 2.0 %copy.13.refs_6_ = f32[64,12,12]{2,1,0:T(8,128)} copy(f32[64,12,12]{0,2,1:T(8,128)} %param.13) | data formatting | bytes 73728 | tf_op args[6]
  4.9 76.0 %shard_map.73 = f32[13,13,7,128]{3,2,1,0:T(8,128)} custom-call(f32[13,13,7,128]{3,2,1,0:T(8,128)} %refs_0_.1, bf16[343,343]{1,0:T(8,128)(2,1)} %refs_1_.1, f32[343,4]{1,0:T(8,128)} %copy.11.refs_2_, bf16[343,1536]{1,0:T(8,128)(2,1)} %bitcast.5, s32[16,32]{1,0:T(8,128)} %bitcast.6, s32[32,4]{1,0:T(8,128)} %copy.12.refs_5_, f32[64,12,12]{2,1,0:T(8,128)} %copy.13.refs_6_), custom_call_target="tpu_custom_call" | custom-call | tf_op jit(solution)/shard_map/pallas_call | solution.py:438
  80.9 2.0 %copy.16 = f32[13,13,7,128]{3,2,1,0:T(8,128)} copy(f32[13,13,7,128]{3,2,1,0:T(8,128)} %shard_map.73) | data formatting | bytes 1211392
  (1 shorter events, 0.0 us)
where the time goes:
time: 83.1 us; the launch traced here: 82.9 us
  Pallas kernels  76 us (91%)
  local copies, waits for them, and re-layouts  6.13 us (7%)
    pallas_call x1, Pallas kernels, local(): pl.pallas_call(kernel, out_shape=jax.ShapeDtypeStruct(parts.shape, F32),...  76 us
    unnamed x2, local copies, waits for them, and re-layouts  3.95 us

commit v1 on v0

--- a/solution.py
+++ b/solution.py
@@ -78,14 +78,16 @@
     return jnp.where(mask, 1.0, 0.0).astype(BF)
 
 
-def body(sizes, parts, amat, pot, proj, atoms, cells, coup, out,
+def body(sizes, parts_in, amat_in, pot_in, proj_in, atoms_in, cells_in, coup_in, out,
+         parts, amat, pot, proj, atoms, cells, coup, load_sem,
          zbuf, field, ybuf, xcat, qt, q, a2, vloc, gmat, csc,
+         expand, pattern, owner, rows_bf,
          part_send, part_recv, coef_send, coef_recv, halo_send, halo_recv,
          hsend_sem, hrecv_sem, psend_sem, precv_sem, csend_sem, crecv_sem):
     ngx, ngy, ngz = sizes
     ix, iy, iz = lax.axis_index("gx"), lax.axis_index("gy"), lax.axis_index("gz")
     cap = POS // ngz
-    own = coup.shape[0] // ngz
+    own = coup.shape[2] // ngz
     chunk = cap * SLOT
 
     def exists(d, sign):
@@ -121,9 +123,18 @@
 
     n_greet = span(ix, ngx) * span(iy, ngy) * span(iz, ngz) - 1 + ngz - 1
 
+    loads = [
+        pltpu.make_async_copy(src, dst, load_sem.at[k])
+        for k, (src, dst) in enumerate((
+            (parts_in, parts), (amat_in, amat), (pot_in, pot), (atoms_in, atoms),
+            (cells_in, cells), (coup_in, coup), (proj_in, proj)))]
+    for load in loads:
+        load.start()
+
     zero8 = jnp.zeros((SUB, LANES), F32)
     field[FIELD:, :] = jnp.zeros((TALL - FIELD, LANES), F32)
     ybuf[...] = jnp.zeros(ybuf.shape, F32)
+    loads[0].wait()
 
     def take(u, carry):
         for v in range(WIDE):
@@ -255,88 +266,96 @@
         return rows
 
     pack()
-    pl.semaphore_wait(barrier, n_greet)
-    halo_start(0)
 
     r_i, n_i = iota((KPAD, NODES), 0), iota((KPAD, NODES), 1)
-    expand = onehot(jnp.logical_and(
+    expand[...] = onehot(jnp.logical_and(
         jnp.logical_and(r_i < EDGE * EDGE * SUB, (r_i & 7) < EDGE),
         n_i == (r_i >> 3) * EDGE + (r_i & 7)))
-    short = expand[:CROWS]
-    a2[...] = dot_nt(dot(short, amat[...]).astype(BF), expand).astype(BF)
-
-    wide_pot = jnp.concatenate(
-        [jnp.broadcast_to(pot[:, g:g + 1], (NODES, LANES)) for g in range(CELLS)], axis=1)
-    v_cells = jnp.dot(short.astype(F32), wide_pot, precision=lax.Precision.HIGHEST,
-                      preferred_element_type=F32)
-    for u, row in enumerate(join_cells(
-            [v_cells[:, g * LANES:(g + 1) * LANES] for g in range(CELLS)])):
-        vloc[pl.ds(u * ROW, ROW), :] = row
+    for load in loads[1:]:
+        load.wait()
+    a2[...] = dot_nt(dot(expand[:CROWS, :], amat[...]).astype(BF), expand[...]).astype(BF)
+
+    vloc[...] = jnp.zeros(vloc.shape, F32)
+    for g in range(CELLS):
+        row = pot[g // 2, g % 2]
+        high = row.astype(BF)
+        low = (row - high.astype(F32)).astype(BF)
+        block = sum(
+            dot_nt(expand[:CROWS, :], jnp.broadcast_to(part, (LANES, NODES)))
+            for part in (high, low))
+        for a in range(EDGE):
+            at = pl.ds((ORDER * (g // 2) + a) * ROW + ORDER * SUB * (g % 2), EDGE * SUB)
+            vloc[at, :] = vloc[at, :] + block[a * EDGE * SUB:(a + 1) * EDGE * SUB]
 
     width = POS * BLK * PA
     s_i, col = iota((POS, width), 0), iota((POS, width), 1)
-    cell_f = cells[...].astype(F32)
-    cell_col = jnp.zeros((1, width), F32)
-    for b in range(BLK):
-        start = s_i * (BLK * PA) + b * PA
-        inside = jnp.logical_and(col >= start, col < start + PA)
-        cell_col = cell_col + jnp.sum(
-            jnp.where(inside, jnp.broadcast_to(cell_f[:, b:b + 1], (POS, width)), 0.0),
-            axis=0, keepdims=True)
     in_slot = onehot(jnp.logical_and(col >= s_i * (BLK * PA), col < (s_i + 1) * (BLK * PA)))
     atom_bf = atoms[...].astype(F32).astype(BF)
     atom_all = dot(atom_bf, in_slot)
     atom_col = jnp.sum(jnp.where(iota((ngz, width), 0) == iz, atom_all, 0.0),
                        axis=0, keepdims=True)
-
-    wide_proj = dot(expand, proj[...])
-    rr, rc = iota((PGROUP, GROUP), 0), iota((PGROUP, GROUP), 1)
-    tr, tc = iota((GROUP, PGROUP), 1), iota((GROUP, PGROUP), 0)
-
-    def merge(row, column):
-        base = (column >> 4) * (BLK * PA) + (column & 15)
-        hit = row == base
-        for b in range(1, BLK):
-            hit = jnp.logical_or(hit, row == base + b * PA)
-        return onehot(jnp.logical_and(hit, (column & 15) < PA))
-
-    narrow, narrow_t = merge(rr, rc), merge(tr, tc)
-    for g in range(CELLS):
-        live = jnp.logical_and(cell_col == g, atom_col >= 0.0)
-        masked = jnp.where(live, wide_proj, 0.0).astype(BF)
-        for k in range(POS // 8):
-            piece = masked[:, k * PGROUP:(k + 1) * PGROUP]
-            q[pl.ds(g * CROWS, CROWS), pl.ds(k * GROUP, GROUP)] = dot(
-                piece[:CROWS], narrow).astype(BF)
-            qt[pl.ds(k * GROUP, GROUP), pl.ds(g * KPAD, KPAD)] = dot_nt(
-                narrow_t, piece).astype(BF)
+    cell_all = dot(cells[...].astype(F32).astype(BF), in_slot)
+    b_i, c_i = iota((BLK, width), 0), iota((BLK, width), 1)
+    slot_of = ((c_i >> 4) * 43691) >> 17
+    block_of = (((c_i - slot_of * (BLK * PA)) >> 2) * 43691) >> 17
+    cell_col = jnp.sum(jnp.where(b_i == block_of, cell_all, 0.0), axis=0, keepdims=True)
+    owner[...] = jnp.broadcast_to(
+        jnp.where(atom_col >= 0.0, cell_col, -1.0), owner.shape)
+
+    pr, pc = iota((KPAD, PGROUP), 0), iota((KPAD, PGROUP), 1)
+    base = ((pr >> 4) & 7) * (BLK * PA) + (pr & 15)
+    hit = pc == base
+    for b in range(1, BLK):
+        hit = jnp.logical_or(hit, pc == base + b * PA)
+    pattern[...] = onehot(jnp.logical_and(hit, (pr & 15) < PA))
+
+    pl.semaphore_wait(barrier, n_greet)
+    halo_start(0)
+
+    def merge(k, carry):
+        columns = pl.ds(pl.multiple_of(k * PGROUP, LANES), PGROUP)
+        rows_bf[...] = dot(expand[...], proj[:, columns]).astype(BF)
+        cell_g = (iota((KPAD, PGROUP), 0) >> 7).astype(F32)
+        chosen = jnp.where(jnp.broadcast_to(owner[0:1, columns], (KPAD, PGROUP)) == cell_g,
+                           pattern[...].astype(F32), 0.0).astype(BF)
+        tall = dot_nt(chosen, rows_bf[...]).astype(BF)
+        wide = dot_nt(rows_bf[:CROWS, :], chosen).astype(BF)
+        to = pl.ds(pl.multiple_of(k * GROUP, GROUP), GROUP)
+        for g in range(CELLS):
+            qt[to, g * KPAD:(g + 1) * KPAD] = tall[g * GROUP:(g + 1) * GROUP]
+            q[g * CROWS:(g + 1) * CROWS, to] = wide[:, g * GROUP:(g + 1) * GROUP]
+        return carry
+
+    lax.fori_loop(0, POS // 8, merge, 0)
 
     at_s, at_c = iota((POS, COLS), 0), iota((POS, COLS), 1)
-    j_c = lax.rem(at_c >> 4, cap)
-    src = onehot(at_s == iz * cap + j_c)
-    got_atoms = dot(atom_bf, src)
+    j_c = (at_c >> 4) & (cap - 1)
+    got_atoms = dot(atom_bf, onehot(at_s == iz * cap + j_c))
     k_r, k_c = iota((ngz, COLS), 0), iota((ngz, COLS), 1)
     here = jnp.logical_and(k_c >= k_r * chunk, k_c < (k_r + 1) * chunk)
     atom_row = jnp.sum(jnp.where(here, got_atoms, 0.0), axis=0, keepdims=True)
     m_r, m_c = iota((LANES, COLS), 0), iota((LANES, COLS), 1)
-    same = jnp.logical_and((m_r & 15) == (m_c & 15), (m_r & 15) < PA)
-    number = (m_r >> 4).astype(F32)
+    same = jnp.logical_and((m_r >> 3) == (m_c & 15), (m_r >> 3) < PA)
+    number = (m_r & 7).astype(F32)
     base_atom = (iz * own).astype(F32)
     member = onehot(jnp.logical_and(
         same, jnp.broadcast_to(atom_row, (LANES, COLS)) - base_atom == number))
     member_t = dot_nt(onehot(iota((COLS, COLS), 0) == iota((COLS, COLS), 1)),
                       member).astype(BF)
+    atoms_here = coup.shape[2]
+    pick = onehot(iota((SUB, atoms_here), 1) == iz * own + iota((SUB, atoms_here), 0))
+    c_r, c_c = iota((LANES, LANES), 0), iota((LANES, LANES), 1)
+    spread = onehot(jnp.logical_and(c_r == (c_c >> 3), (c_c >> 3) < PA))
+    diagonal = (c_r & 7) == (c_c & 7)
     csc[...] = jnp.zeros(csc.shape, F32)
-    for m in range(own):
-        csc[pl.ds(m * SLOT, PA), pl.ds(0, PA)] = coup[iz * own + m]
-    c_r, c_c = iota((LANES, LANES), 0), iota((LANES, LANES), 1)
-    spread = onehot(jnp.logical_and(c_r == (c_c & 15), (c_c & 15) < PA))
-    diagonal = (c_r >> 4) == (c_c >> 4)
-    whole = csc[...]
-    high = whole.astype(BF)
-    low = (whole - high.astype(F32)).astype(BF)
-    for h, piece in enumerate((high, low)):
-        block = jnp.where(diagonal, dot(piece, spread), 0.0).astype(BF)
+    for h in range(2):
+        for t in range(PA):
+            part = coup[t]
+            high = part.astype(BF)
+            if h:
+                high = (part - high.astype(F32)).astype(BF)
+            csc[t * SUB:(t + 1) * SUB, 0:PA] = dot_nt(pick, high)
+        block = jnp.where(diagonal, dot(csc[...].astype(BF), spread), 0.0).astype(BF)
         gmat[h] = dot(dot(member_t, block).astype(BF), member).astype(BF)
 
     xcat[CROWS:, :] = jnp.zeros((KPAD - CROWS, CELLS * LANES), BF)
@@ -432,15 +451,25 @@
     def kernel(*refs):
         body(sizes, *refs)
 
+    args = (
+        parts,
+        cell_matrix,
+        jnp.transpose(cell_potential, (1, 2, 3, 0)),
+        projectors.reshape(NODES, POS * BLK * PA),
+        slot_atom.reshape(ngz, POS),
+        jnp.transpose(slot_cells.reshape(POS, BLK)),
+        jnp.transpose(coupling, (1, 2, 0)),
+    )
     vm = pltpu.VMEM
     dma = pltpu.SemaphoreType.DMA
     n = len(DIRS)
     return pl.pallas_call(
         kernel,
         out_shape=jax.ShapeDtypeStruct(parts.shape, F32),
-        in_specs=[pl.BlockSpec(memory_space=pltpu.VMEM)] * 7,
+        in_specs=[pl.BlockSpec(memory_space=pl.ANY)] * 7,
         out_specs=pl.BlockSpec(memory_space=pltpu.VMEM),
-        scratch_shapes=[
+        scratch_shapes=[vm(a.shape, a.dtype) for a in args] + [
+            dma((7,)),
             vm((2, FIELD, LANES), F32),
             vm((TALL, LANES), F32),
             vm((2 * LANES, LANES), F32),
@@ -451,6 +480,10 @@
             vm((FIELD, LANES), F32),
             vm((2, COLS, COLS), BF),
             vm((LANES, LANES), F32),
+            vm((KPAD, NODES), BF),
+            vm((KPAD, PGROUP), BF),
+            vm((SUB, POS * BLK * PA), F32),
+            vm((KPAD, PGROUP), BF),
             vm((COLS, LANES), BF),
             vm((COLS, LANES), BF),
             vm((COLS, LANES), BF),
@@ -466,15 +499,7 @@
         ],
         compiler_params=pltpu.CompilerParams(
             collective_id=0, has_side_effects=True, vmem_limit_bytes=56 * 1024 * 1024),
-    )(
-        parts,
-        cell_matrix,
-        cell_potential.reshape(NODES, CELLS),
-        projectors.reshape(NODES, POS * BLK * PA),
-        slot_atom.reshape(ngz, POS),
-        slot_cells.reshape(POS, BLK),
-        coupling,
-    )
+    )(*args)
 
 
 def solution(mesh):

time: 83.1 us -> 75.7 us (0.911)
  local copies, waits for them, and re-layouts: 6.13 us -> 1.99 us
  Pallas kernels: 76 us -> 73.3 us
    pallas_call x1, Pallas kernels: 76 us -> 73.3 us  [local(): pl.pallas_call(kernel, out_shape=jax.ShapeDtypeStruct(parts.shape, F32),...]
    reshape x3 -> x0, local copies, waits for them, and re-layouts: 2.18 us -> none  [the longest x1 1.36 us: local(): slot_cells.reshape(POS, BLK)]
    unnamed x2 -> x1, local copies, waits for them, and re-layouts: 3.95 us -> 1.99 us
where the time goes in v1:
time: 75.7 us; the launch traced here: 75.3 us
  Pallas kernels  73.3 us (97%)
  local copies, waits for them, and re-layouts  1.99 us (3%)
    pallas_call x1, Pallas kernels, local(): pl.pallas_call(kernel, out_shape=jax.ShapeDtypeStruct(parts.shape, F32),...  73.3 us
    unnamed x1, local copies, waits for them, and re-layouts  1.99 us

profile of v1, /device:TPU:1, one launch (start us, length us, event | category | flops | bytes accessed | tf_op | source)
XLA Modules:
  0.0 75.3 jit_solution(7238852329357101731)
XLA Ops:
  0.0 73.3 %shard_map.73 = f32[13,13,7,128]{3,2,1,0:T(8,128)} custom-call(f32[13,13,7,128]{3,2,1,0:T(8,128)} %refs_0_.1, bf16[343,343]{1,0:T(8,128)(2,1)} %refs_1_.1, f32[2,2,1,343]{3,2,1,0:T(1,128)} %bitcast.10, bf16[343,1536]{1,0:T(8,128)(2,1)} %bitcast.7, s32[16,32]{1,0:T(8,128)} %bitcast.9, s32[4,32]{1,0:T(4,128)} %bitcast.11, f32[12,12,64]{2,1,0:T(8,128)} %bitcast.8), custom_call_target="tpu_custom_call" | custom-call | tf_op jit(solution)/shard_map/pallas_call | solution.py:466
  73.3 2.0 %copy.9 = f32[13,13,7,128]{3,2,1,0:T(8,128)} copy(f32[13,13,7,128]{3,2,1,0:T(8,128)} %shard_map.73) | data formatting | bytes 1211392
